TPU v7x, 256 devices: a whole 4x4x8 slice. The times are simulated.
256 devices in a mesh: tok: 16 (over y, x), col: 16 (over z, core).
Axes of the slice: x: 4, y: 4, z: 8, core: 2. Of those that a mesh axis runs over, the one named last changes fastest.
Arguments:
- activations: bfloat16 [32768, 8192], P('tok', 'col'), may hold values from -60 to 60, as said below
- weight: bfloat16 [8192, 8192], P('tok', 'col'), may hold values from -6 to 6
- keep_mask: int32 [8192, 8192], P('tok', 'col'), may hold values from 0 to 1
Outputs:
- new_weight: bfloat16 [8192, 8192], P('tok', 'col')
Inputs may be any that keep to these rules, and one draw needn't show every extreme that they name: activations of calibration tokens.
All inputs are finite; a program needn't handle non-finite values.
Results may differ from a plain program's by a relative error of at most 0.00115.
Values may be sent and summed in bfloat16 or wider, within the bound.
A program may use at most 64 MiB of HBM per device.

v0:
```python
import jax
import jax.numpy as jnp
from jax import lax
from jax.sharding import PartitionSpec as P

B = 1024
ITERS = 4


def split(x):
    high = lax.reduce_precision(x, exponent_bits=8, mantissa_bits=7)
    return (high.astype(jnp.bfloat16), (x - high).astype(jnp.bfloat16))


def mm(a, b, dims=(((1,), (0,)), ((), ()))):
    return lax.dot_general(a, b, dims, preferred_element_type=jnp.float32)


def per_device(activations, weight, keep_mask):
    n_col = lax.axis_size("col")
    n_tok = lax.axis_size("tok")
    tok_rows = activations.shape[0]
    panel_width = B // n_col
    total_count = tok_rows * n_tok
    pruned = jnp.where(
        keep_mask[:, :panel_width] == 0, weight[:, :panel_width], jnp.zeros((), jnp.bfloat16)
    )
    panel = lax.all_gather(activations[:, :panel_width], "col", axis=1, tiled=True)
    partial_panel = mm(activations, panel, (((0,), (0,)), ((), ())))
    pruned_panel = lax.all_gather(pruned, "col", axis=1, tiled=True)
    hessian_panel = lax.psum(partial_panel, "tok") / total_count
    block = lax.all_gather(hessian_panel[:panel_width], "col", axis=0, tiled=True)
    rows = lax.broadcasted_iota(jnp.int32, (B, B), 0)
    columns = lax.broadcasted_iota(jnp.int32, (B, B), 1)
    on_diagonal = rows == columns
    mean_diagonal = jnp.sum(jnp.where(on_diagonal, block, 0.0)) / B
    damped = block + jnp.where(on_diagonal, 0.01 * mean_diagonal, 0.0)
    scale = lax.rsqrt(jnp.sum(damped * damped))
    g = damped * scale
    y = pruned_panel.astype(jnp.float32)
    for sweep in range(ITERS):
        g_high = g.astype(jnp.bfloat16)
        y_high, y_low = split(y)
        y = 2.0 * y - (mm(y_high, g_high) + mm(y_low, g_high))
        if sweep < ITERS - 1:
            g = 2.0 * g - mm(g_high, g_high)
    y_high, y_low = split(y * scale)
    h_high, h_low = split(hessian_panel)
    nt = (((1,), (1,)), ((), ()))
    correction = mm(y_high, h_high, nt) + mm(y_low, h_high, nt) + mm(y_high, h_low, nt)
    kept = keep_mask.astype(jnp.float32)
    return (kept * (weight.astype(jnp.float32) - correction)).astype(jnp.bfloat16)


def solution(mesh):
    return jax.shard_map(
        per_device,
        mesh=mesh,
        in_specs=(P("tok", "col"), P("tok", "col"), P("tok", "col")),
        out_specs=P("tok", "col"),
        check_vma=False,
    )
```

profile of v0, /device:TPU:1, one launch (start us, length us, event | category | flops | bytes accessed | tf_op | source)
XLA Modules:
  0.0 284.6 jit_solution(3406045359667828655)
XLA Ops:
  6.5 0.0 all-gather.6.cloned.1.call-start
  6.5 1.2 slice.14
  7.8 0.9 copy.10
  8.7 0.0 all-gather.6.cloned.1.call-update
  8.7 0.0 all-reduce.2.cloned.1.call-start
  8.7 46.8 %all-gather.6.cloned.1.call-done = bf16[2048,1024]{0,1:T(8,128)(2,1)} async-done(((bf16[2048,64]{0,1:T(8,128)(2,1)}), bf16[2048,1024]{0,1:T(8,128)(2,1)}) %all-gather.6.cloned.1.call-update) | async-done | bytes 4194320 | tf_op jit(solution)/shard_map/all_gather | solution.py:28
  55.5 0.0 copy-done.4
  55.6 5.9 %fusion.29 = f32[512,1024]{1,0:T(8,128)} fusion(bf16[2048,512]{1,0:T(8,128)(2,1)S(1)} %copy-done.4, bf16[2048,1024]{0,1:T(8,128)(2,1)} %all-gather.6.cloned.1.call-done), kind=kOutput, calls=%fused_computation.50 | convolution fusion | flops 2147483648 | bytes 8388608 | tf_op jit(solution)/shard_map/dot_general | solution.py:16
  61.5 0.0 all-reduce.2.cloned.1.call-update
  61.5 0.0 all-gather.4.cloned.1.call-start
  61.5 0.8 slice-done.1
  62.4 0.1 copy.9
  62.5 0.0 slice-done
  62.5 0.1 copy.8
  62.6 0.6 compare_select_fusion
  63.2 0.0 all-gather.4.cloned.1.call-update
  63.3 0.0 all-gather.8.cloned.1.call-start
  63.3 95.8 %all-reduce.2.cloned.1.call-done = f32[512,1024]{1,0:T(8,128)} async-done(((f32[512,1024]{1,0:T(8,128)}), f32[512,1024]{1,0:T(8,128)}) %all-reduce.2.cloned.1.call-update) | async-done | bytes 2097168 | tf_op jit(solution)/shard_map/psum | solution.py:31
  159.1 1.8 broadcast_multiply_fusion
  160.9 0.7 slice.16
  161.6 0.0 all-gather.8.cloned.1.call-update
  161.6 39.0 %all-gather.4.cloned.1.call-done = bf16[512,1024]{0,1:T(8,128)(2,1)} async-done(((bf16[512,64]{0,1:T(8,128)(2,1)}), bf16[512,1024]{0,1:T(8,128)(2,1)}) %all-gather.4.cloned.1.call-update) | async-done | bytes 1048592 | tf_op jit(solution)/shard_map/all_gather | solution.py:30
  200.6 1.7 copy.6
  202.3 41.0 %all-gather.8.cloned.1.call-done = f32[1024,1024]{1,0:T(8,128)} async-done(((f32[64,1024]{1,0:T(8,128)}), f32[1024,1024]{1,0:T(8,128)}) %all-gather.8.cloned.1.call-update) | async-done | bytes 4194320 | tf_op jit(solution)/shard_map/all_gather | solution.py:32
  243.3 2.9 %select_reduce_fusion = f32[]{:T(128)} fusion(f32[1024,1024]{1,0:T(8,128)} %all-gather.8.cloned.1.call-done), kind=kLoop, calls=%fused_computation.5 | loop fusion | flops 3145727 | bytes 4194308 | tf_op jit(solution)/shard_map/reduce_sum | solution.py:36
  246.9 3.9 %multiply_reduce_fusion = f32[]{:T(128)} fusion(f32[1024,1024]{1,0:T(8,128)} %all-gather.8.cloned.1.call-done, f32[]{:T(128)S(6)} %mul_shard_map.3), kind=kLoop, calls=%fused_computation.3 | loop fusion | flops 5242879 | bytes 4194312 | tf_op jit(solution)/shard_map/reduce_sum | solution.py:38
  251.4 7.0 %multiply_subtract_fusion.1 = f32[1024,1024]{1,0:T(8,128)S(1)} fusion(f32[1024,1024]{1,0:T(8,128)} %all-gather.8.cloned.1.call-done, f32[]{:T(128)S(6)} %rsqrt.3, f32[]{:T(128)S(6)} %mul_shard_map.3), kind=kOutput, calls=%fused_computation.2 | convolution fusion | flops 2159017984 | bytes 8388616 | tf_op jit(solution)/shard_map/dot_general | solution.py:16
  258.5 0.0 copy-start.1
  258.5 2.3 multiply_subtract_fusion
  260.8 0.0 copy-done.1
  260.8 1.3 fusion.20
  262.1 1.4 fusion.6
  263.5 1.3 fusion.17
  264.8 1.3 add_subtract_fusion.1
  266.2 2.4 subtract_convert_fusion
  268.5 1.3 fusion.18
  269.8 1.6 add_subtract_fusion
  271.5 1.3 fusion.19
  272.7 0.0 copy-start
  272.7 1.4 subtract_multiply_fusion
  274.1 0.2 copy-done
  274.3 0.7 fusion.22
  275.1 0.0 copy-start.2
  275.1 0.0 copy-start.3
  275.1 0.7 convolution_add_fusion.1
  275.9 0.4 copy-done.2
  276.3 0.1 copy-done.3
  276.4 1.6 fusion.10
  (3 shorter events, 0.0 us)
Async XLA Ops:
  6.5 49.0 %copy-start.4 = (bf16[2048,512]{1,0:T(8,128)(2,1)S(1)}, bf16[2048,512]{1,0:T(8,128)(2,1)}, u32[]{:S(2)}) copy-start(bf16[2048,512]{1,0:T(8,128)(2,1)} %param.3) | copy-start | bytes 6291460
  6.5 49.0 %all-gather.6.cloned.1.call-start = ((), (), s32[]{:S(2)}) async-start(), calls=%async_computation.1 | async-start | bytes 4456448 | tf_op jit(solution)/shard_map/all_gather | solution.py:28
  8.7 150.4 %all-reduce.2.cloned.1.call-start = ((), (), s32[]{:S(2)}) async-start(), calls=%async_computation.2 | async-start | bytes 4194304 | tf_op jit(solution)/shard_map/psum | solution.py:31
  61.5 0.9 slice-start.1
  61.5 1.0 slice-start
  61.5 139.1 %all-gather.4.cloned.1.call-start = ((), (), s32[]{:S(2)}) async-start(), calls=%async_computation | async-start | bytes 1114112 | tf_op jit(solution)/shard_map/all_gather | solution.py:30
  63.3 180.0 %all-gather.8.cloned.1.call-start = ((), (), s32[]{:S(2)}) async-start(), calls=%async_computation.3 | async-start | bytes 4456448 | tf_op jit(solution)/shard_map/all_gather | solution.py:32
  258.5 2.4 copy-start.1
  272.7 1.6 copy-start
  275.1 1.2 copy-start.2
  275.1 1.3 copy-start.3
Sparse Core Ops, SparseCore 0:
  9.2 46.3 all-gather.5
  61.6 97.4 all-reduce.1
  161.1 39.5 all-gather.3
  202.4 40.7 all-gather.7
where the time goes:
time: 285 us
  waiting for transfers between devices  223 us (78%)
  matrix products  31.6 us (11%)
  between operations  14.6 us (5%)
  other arithmetic  9.21 us (3%)
  local copies, waits for them, and re-layouts  6.38 us (2%)
    psum x1, waiting for transfers between devices, per_device(): hessian_panel = lax.psum(partial_panel, 'tok') / total_count  95.8 us
    all_gather x1, waiting for transfers between devices, per_device(): lax.all_gather(activations[:, :panel_width], 'col', axis=1, tiled=True)  46.8 us
    all_gather x1, waiting for transfers between devices, per_device(): lax.all_gather(hessian_panel[:panel_width], 'col', axis=0, tiled=True)  41 us
    all_gather x1, waiting for transfers between devices, per_device(): pruned_panel = lax.all_gather(pruned, 'col', axis=1, tiled=True)  39 us
    dot_general x15, matrix products, mm(): return lax.dot_general(a, b, dims, preferred_element_type=jnp.float32)  31.6 us
  transfers between devices with their start and end apart: 4, of which 4 were waited for; matrix products, arithmetic and copies ran while one was open for 2% of the time, Pallas kernels for 0%

commit v1 on v0

--- a/solution.py
+++ b/solution.py
@@ -27,7 +27,12 @@
     )
     panel = lax.all_gather(activations[:, :panel_width], "col", axis=1, tiled=True)
     partial_panel = mm(activations, panel, (((0,), (0,)), ((), ())))
-    pruned_panel = lax.all_gather(pruned, "col", axis=1, tiled=True)
+    ring = [pruned]
+    for hop in range(15):
+        ring.append(lax.ppermute(ring[-1], "col", [(dev, (dev + 1) % 16) for dev in range(16)]))
+    pruned_panel = jnp.roll(
+        jnp.concatenate(ring[::-1], axis=1), (lax.axis_index("col") + 1) * ring[0].shape[1], axis=1
+    )
     hessian_panel = lax.psum(partial_panel, "tok") / total_count
     block = lax.all_gather(hessian_panel[:panel_width], "col", axis=0, tiled=True)
     rows = lax.broadcasted_iota(jnp.int32, (B, B), 0)

time: 285 us -> 310 us (1.088); the launches traced: 285 us -> 305 us
  starting transfers between devices: 0.13 us -> 13.5 us
  local copies, waits for them, and re-layouts: 6.38 us -> 17.5 us
  waiting for transfers between devices: 223 us -> 218 us
    ppermute x0 -> x15, waiting for transfers between devices: none -> 73.9 us  [per_device(): lax.ppermute(ring[-1], 'col', [(dev, (dev + 1) % 16) for dev in range(16)])]
    all_gather x1, waiting for transfers between devices: 41 us -> 0.02 us  [per_device(): lax.all_gather(hessian_panel[:panel_width], 'col', axis=0, tiled=True)]
    all_gather x1 -> x0, waiting for transfers between devices: 39 us -> none  [per_device(): pruned_panel = lax.all_gather(pruned, 'col', axis=1, tiled=True)]
    ppermute x0 -> x15, starting transfers between devices: none -> 13.5 us  [per_device(): lax.ppermute(ring[-1], 'col', [(dev, (dev + 1) % 16) for dev in range(16)])]
    unnamed x13 -> x35, local copies, waits for them, and re-layouts: 1.93 us -> 9.33 us
    concatenate x0 -> x1, local copies, waits for them, and re-layouts: none -> 6.18 us  [per_device(): jnp.roll(jnp.concatenate(ring[::-1], axis=1), (lax.axis_index('col') + 1)...]
  transfers between devices with their start and end apart: 4 -> 18, of which waited for: 4 -> 17; matrix products, arithmetic and copies ran while one was open for 2% -> 2% of each run, Pallas kernels for 0% -> 0%
where the time goes in v1:
time: 310 us; the launch traced here: 305 us
  waiting for transfers between devices  218 us (70%)
  matrix products  31.7 us (10%)
  local copies, waits for them, and re-layouts  17.5 us (6%)
  between operations  14.6 us (5%)
  starting transfers between devices  13.5 us (4%)
  other arithmetic  9.52 us (3%)
    psum x1, waiting for transfers between devices, per_device(): hessian_panel = lax.psum(partial_panel, 'tok') / total_count  97.5 us
    ppermute x15, waiting for transfers between devices, per_device(): lax.ppermute(ring[-1], 'col', [(dev, (dev + 1) % 16) for dev in range(16)])  73.9 us
    all_gather x1, waiting for transfers between devices, per_device(): lax.all_gather(activations[:, :panel_width], 'col', axis=1, tiled=True)  46.8 us
    dot_general x15, matrix products, mm(): return lax.dot_general(a, b, dims, preferred_element_type=jnp.float32)  31.7 us
    ppermute x15, starting transfers between devices, per_device(): lax.ppermute(ring[-1], 'col', [(dev, (dev + 1) % 16) for dev in range(16)])  13.5 us
    unnamed x35, local copies, waits for them, and re-layouts  9.33 us
  transfers between devices with their start and end apart: 18, of which 17 were waited for; matrix products, arithmetic and copies ran while one was open for 2% of the time, Pallas kernels for 0%

profile of v1, /device:TPU:1, one launch (start us, length us, event | category | flops | bytes accessed | tf_op | source)
XLA Modules:
  0.0 305.2 jit_solution(6890654147600935636)
XLA Ops:
  6.5 1.2 slice.14
  7.8 0.9 copy.5
  8.7 46.8 %all-gather.3.cloned.1.call-done = bf16[2048,1024]{0,1:T(8,128)(2,1)} async-done(((bf16[2048,64]{0,1:T(8,128)(2,1)}), bf16[2048,1024]{0,1:T(8,128)(2,1)}) %all-gather.3.cloned.1.call-update) | async-done | bytes 4194320 | tf_op jit(solution)/shard_map/all_gather | solution.py:28
  55.6 6.0 %fusion.34 = f32[512,1024]{1,0:T(8,128)} fusion(bf16[2048,512]{1,0:T(8,128)(2,1)S(1)} %copy-done.16, bf16[2048,1024]{0,1:T(8,128)(2,1)} %all-gather.3.cloned.1.call-done), kind=kOutput, calls=%fused_computation.55 | convolution fusion | flops 2147483648 | bytes 8388608 | tf_op jit(solution)/shard_map/dot_general | solution.py:16
  61.6 97.5 %all-reduce.2.cloned.1.call-done = f32[512,1024]{1,0:T(8,128)} async-done(((f32[512,1024]{1,0:T(8,128)}), f32[512,1024]{1,0:T(8,128)}) %all-reduce.2.cloned.1.call-update) | async-done | bytes 2097168 | tf_op jit(solution)/shard_map/psum | solution.py:36
  159.1 1.8 broadcast_multiply_fusion
  160.9 0.7 slice.16
  161.7 0.9 fusion.25
  162.6 2.9 collective-permute-start
  165.6 1.9 collective-permute-done
  167.5 2.4 collective-permute-start.1
  170.0 1.9 collective-permute-done.1
  171.9 2.4 collective-permute-start.2
  174.4 3.4 %collective-permute-done.2 = bf16[512,64]{1,0:T(8,128)(2,1)S(1)} collective-permute-done((bf16[512,64]{1,0:T(8,128)(2,1)S(1)}, bf16[512,64]{1,0:T(8,128)(2,1)S(1)}, u32[]{:S(2)}, u32[]{:S(2)}) %collective-permute-start.2) | collective-permute-done | bytes 65568 | tf_op jit(solution)/shard_map/ppermute | solution.py:32
  177.8 0.7 copy-done.4
  178.4 2.4 collective-permute-start.3
  180.8 4.1 %collective-permute-done.3 = bf16[512,64]{1,0:T(8,128)(2,1)S(1)} collective-permute-done((bf16[512,64]{1,0:T(8,128)(2,1)S(1)}, bf16[512,64]{1,0:T(8,128)(2,1)S(1)}, u32[]{:S(2)}, u32[]{:S(2)}) %collective-permute-start.3) | collective-permute-done | bytes 65568 | tf_op jit(solution)/shard_map/ppermute | solution.py:32
  184.9 0.7 copy-done.5
  185.6 2.5 collective-permute-start.4
  188.1 5.0 %collective-permute-done.4 = bf16[512,64]{1,0:T(8,128)(2,1)S(1)} collective-permute-done((bf16[512,64]{1,0:T(8,128)(2,1)S(1)}, bf16[512,64]{1,0:T(8,128)(2,1)S(1)}, u32[]{:S(2)}, u32[]{:S(2)}) %collective-permute-start.4) | collective-permute-done | bytes 65568 | tf_op jit(solution)/shard_map/ppermute | solution.py:32
  193.7 0.7 collective-permute-start.5
  194.4 7.3 %collective-permute-done.5 = bf16[512,64]{1,0:T(8,128)(2,1)S(1)} collective-permute-done((bf16[512,64]{1,0:T(8,128)(2,1)S(1)}, bf16[512,64]{1,0:T(8,128)(2,1)S(1)}, u32[]{:S(2)}, u32[]{:S(2)}) %collective-permute-start.5) | collective-permute-done | bytes 65568 | tf_op jit(solution)/shard_map/ppermute | solution.py:32
  202.4 6.0 %collective-permute-done.6 = bf16[512,64]{1,0:T(8,128)(2,1)S(1)} collective-permute-done((bf16[512,64]{1,0:T(8,128)(2,1)S(1)}, bf16[512,64]{1,0:T(8,128)(2,1)S(1)}, u32[]{:S(2)}, u32[]{:S(2)}) %collective-permute-start.6) | collective-permute-done | bytes 65568 | tf_op jit(solution)/shard_map/ppermute | solution.py:32
  209.0 5.6 %collective-permute-done.7 = bf16[512,64]{1,0:T(8,128)(2,1)S(1)} collective-permute-done((bf16[512,64]{1,0:T(8,128)(2,1)S(1)}, bf16[512,64]{1,0:T(8,128)(2,1)S(1)}, u32[]{:S(2)}, u32[]{:S(2)}) %collective-permute-start.7) | collective-permute-done | bytes 65568 | tf_op jit(solution)/shard_map/ppermute | solution.py:32
  215.3 5.6 %collective-permute-done.8 = bf16[512,64]{1,0:T(8,128)(2,1)S(1)} collective-permute-done((bf16[512,64]{1,0:T(8,128)(2,1)S(1)}, bf16[512,64]{1,0:T(8,128)(2,1)S(1)}, u32[]{:S(2)}, u32[]{:S(2)}) %collective-permute-start.8) | collective-permute-done | bytes 65568 | tf_op jit(solution)/shard_map/ppermute | solution.py:32
  221.5 5.6 %collective-permute-done.9 = bf16[512,64]{1,0:T(8,128)(2,1)S(1)} collective-permute-done((bf16[512,64]{1,0:T(8,128)(2,1)S(1)}, bf16[512,64]{1,0:T(8,128)(2,1)S(1)}, u32[]{:S(2)}, u32[]{:S(2)}) %collective-permute-start.9) | collective-permute-done | bytes 65568 | tf_op jit(solution)/shard_map/ppermute | solution.py:32
  227.8 5.6 %collective-permute-done.10 = bf16[512,64]{1,0:T(8,128)(2,1)S(1)} collective-permute-done((bf16[512,64]{1,0:T(8,128)(2,1)S(1)}, bf16[512,64]{1,0:T(8,128)(2,1)S(1)}, u32[]{:S(2)}, u32[]{:S(2)}) %collective-permute-start.10) | collective-permute-done | bytes 65568 | tf_op jit(solution)/shard_map/ppermute | solution.py:32
  234.0 5.6 %collective-permute-done.11 = bf16[512,64]{1,0:T(8,128)(2,1)S(1)} collective-permute-done((bf16[512,64]{1,0:T(8,128)(2,1)S(1)}, bf16[512,64]{1,0:T(8,128)(2,1)S(1)}, u32[]{:S(2)}, u32[]{:S(2)}) %collective-permute-start.11) | collective-permute-done | bytes 65568 | tf_op jit(solution)/shard_map/ppermute | solution.py:32
  240.3 5.6 %collective-permute-done.12 = bf16[512,64]{1,0:T(8,128)(2,1)S(1)} collective-permute-done((bf16[512,64]{1,0:T(8,128)(2,1)S(1)}, bf16[512,64]{1,0:T(8,128)(2,1)S(1)}, u32[]{:S(2)}, u32[]{:S(2)}) %collective-permute-start.12) | collective-permute-done | bytes 65568 | tf_op jit(solution)/shard_map/ppermute | solution.py:32
  246.6 5.6 %collective-permute-done.13 = bf16[512,64]{1,0:T(8,128)(2,1)S(1)} collective-permute-done((bf16[512,64]{1,0:T(8,128)(2,1)S(1)}, bf16[512,64]{1,0:T(8,128)(2,1)S(1)}, u32[]{:S(2)}, u32[]{:S(2)}) %collective-permute-start.13) | collective-permute-done | bytes 65568 | tf_op jit(solution)/shard_map/ppermute | solution.py:32
  252.8 5.1 %collective-permute-done.14 = bf16[512,64]{1,0:T(8,128)(2,1)} collective-permute-done((bf16[512,64]{1,0:T(8,128)(2,1)S(1)}, bf16[512,64]{1,0:T(8,128)(2,1)}, u32[]{:S(2)}, u32[]{:S(2)}) %collective-permute-start.14) | collective-permute-done | bytes 65568 | tf_op jit(solution)/shard_map/ppermute | solution.py:32
  257.9 6.2 %concatenate.6 = bf16[512,2048]{1,0:T(8,128)(2,1)S(1)} concatenate(bf16[512,64]{1,0:T(8,128)(2,1)} %collective-permute-done.14, bf16[512,64]{1,0:T(8,128)(2,1)} %copy-done.15, bf16[512,64]{1,0:T(8,128)(2,1)} %copy-done.14, bf16[512,64]{1,0:T(8,128)(2,1)} %copy-done.13, bf16[512,64]{1,0:T(8,128)(2,1)} %copy-done.12, bf16[512,64]{1,0:T(8,128)(2,1)} %copy-done.11, ...), dimensions={1} | concatenate | bytes 4194304 | tf_op jit(solution)/shard_map/jit(_roll_dynamic)/concatenate | solution.py:33
  264.1 2.9 select_reduce_fusion
  267.7 3.9 %multiply_reduce_fusion = f32[]{:T(128)} fusion(f32[1024,1024]{1,0:T(8,128)} %all-gather.5.cloned.1.call-done, f32[]{:T(128)S(6)} %mul_shard_map.3), kind=kLoop, calls=%fused_computation.3 | loop fusion | flops 5242879 | bytes 4194312 | tf_op jit(solution)/shard_map/reduce_sum | solution.py:43
  272.3 7.1 %multiply_subtract_fusion.1 = f32[1024,1024]{1,0:T(8,128)S(1)} fusion(f32[1024,1024]{1,0:T(8,128)} %all-gather.5.cloned.1.call-done, f32[]{:T(128)S(6)} %rsqrt.3, f32[]{:T(128)S(6)} %mul_shard_map.3), kind=kOutput, calls=%fused_computation.2 | convolution fusion | flops 2159017984 | bytes 8388616 | tf_op jit(solution)/shard_map/dot_general | solution.py:16
  279.4 2.3 multiply_subtract_fusion
  281.8 1.4 fusion.11
  283.1 1.5 fusion.6
  284.6 1.3 fusion.17
  285.9 1.3 add_subtract_fusion.1
  287.2 2.3 subtract_convert_fusion
  289.6 1.3 fusion.19
  290.9 1.5 add_subtract_fusion
  292.4 1.3 fusion.20
  293.7 1.3 subtract_multiply_fusion
  295.2 0.7 fusion.24
  296.0 0.8 convolution_add_fusion.1
  297.0 1.6 fusion.10
  (48 shorter events, 7.3 us)
Async XLA Ops:
  6.5 49.0 %copy-start.16 = (bf16[2048,512]{1,0:T(8,128)(2,1)S(1)}, bf16[2048,512]{1,0:T(8,128)(2,1)}, u32[]{:S(2)}) copy-start(bf16[2048,512]{1,0:T(8,128)(2,1)} %param.3) | copy-start | bytes 6291460
  6.5 49.0 %all-gather.3.cloned.1.call-start = ((), (), s32[]{:S(2)}) async-start(), calls=%async_computation | async-start | bytes 4456448 | tf_op jit(solution)/shard_map/all_gather | solution.py:28
  8.7 150.4 %all-reduce.2.cloned.1.call-start = ((), (), s32[]{:S(2)}) async-start(), calls=%async_computation.1 | async-start | bytes 4194304 | tf_op jit(solution)/shard_map/psum | solution.py:36
  61.5 100.1 %copy-start.2 = (s32[512,512]{1,0:T(8,128)S(1)}, s32[512,512]{1,0:T(8,128)}, u32[]{:S(2)}) copy-start(s32[512,512]{1,0:T(8,128)} %param.5) | copy-start | bytes 3145732
  61.5 202.6 %all-gather.5.cloned.1.call-start = ((), (), s32[]{:S(2)}) async-start(), calls=%async_computation.2 | async-start | bytes 4456448 | tf_op jit(solution)/shard_map/all_gather | solution.py:37
  162.6 4.9 %collective-permute-start = (bf16[512,64]{1,0:T(8,128)(2,1)S(1)}, bf16[512,64]{1,0:T(8,128)(2,1)S(1)}, u32[]{:S(2)}, u32[]{:S(2)}) collective-permute-start(bf16[512,64]{1,0:T(8,128)(2,1)S(1)} %fusion.25), channel_id=1, source_target_pairs={{0,1},{1,2},{2,3},{3,4},{4,5},{5,6},{6,7},{7,8},{8,9},{9,10},{10,1... | collective-permute-start | bytes 196616 | tf_op jit(solution)/shard_map/ppermute | solution.py:32
  167.5 4.4 %collective-permute-start.1 = (bf16[512,64]{1,0:T(8,128)(2,1)S(1)}, bf16[512,64]{1,0:T(8,128)(2,1)S(1)}, u32[]{:S(2)}, u32[]{:S(2)}) collective-permute-start(bf16[512,64]{1,0:T(8,128)(2,1)S(1)} %collective-permute-done), channel_id=1, source_target_pairs={{0,1},{1,2},{2,3},{3,4},{4,5},{5,6},{6,7},{7,8},{8,9},{9,10},{10,1... | collective-permute-start | bytes 196616 | tf_op jit(solution)/shard_map/ppermute | solution.py:32
  171.9 5.9 %collective-permute-start.2 = (bf16[512,64]{1,0:T(8,128)(2,1)S(1)}, bf16[512,64]{1,0:T(8,128)(2,1)S(1)}, u32[]{:S(2)}, u32[]{:S(2)}) collective-permute-start(bf16[512,64]{1,0:T(8,128)(2,1)S(1)} %collective-permute-done.1), channel_id=1, source_target_pairs={{0,1},{1,2},{2,3},{3,4},{4,5},{5,6},{6,7},{7,8},{8,9},{9,10},{10,1... | collective-permute-start | bytes 196616 | tf_op jit(solution)/shard_map/ppermute | solution.py:32
  177.8 0.7 copy-start.4
  178.4 6.5 %collective-permute-start.3 = (bf16[512,64]{1,0:T(8,128)(2,1)S(1)}, bf16[512,64]{1,0:T(8,128)(2,1)S(1)}, u32[]{:S(2)}, u32[]{:S(2)}) collective-permute-start(bf16[512,64]{1,0:T(8,128)(2,1)S(1)} %collective-permute-done.2), channel_id=1, source_target_pairs={{0,1},{1,2},{2,3},{3,4},{4,5},{5,6},{6,7},{7,8},{8,9},{9,10},{10,1... | collective-permute-start | bytes 196616 | tf_op jit(solution)/shard_map/ppermute | solution.py:32
  184.9 0.7 copy-start.5
  185.6 7.5 %collective-permute-start.4 = (bf16[512,64]{1,0:T(8,128)(2,1)S(1)}, bf16[512,64]{1,0:T(8,128)(2,1)S(1)}, u32[]{:S(2)}, u32[]{:S(2)}) collective-permute-start(bf16[512,64]{1,0:T(8,128)(2,1)S(1)} %collective-permute-done.3), channel_id=1, source_target_pairs={{0,1},{1,2},{2,3},{3,4},{4,5},{5,6},{6,7},{7,8},{8,9},{9,10},{10,1... | collective-permute-start | bytes 196616 | tf_op jit(solution)/shard_map/ppermute | solution.py:32
  193.1 0.7 copy-start.6
  193.7 8.0 %collective-permute-start.5 = (bf16[512,64]{1,0:T(8,128)(2,1)S(1)}, bf16[512,64]{1,0:T(8,128)(2,1)S(1)}, u32[]{:S(2)}, u32[]{:S(2)}) collective-permute-start(bf16[512,64]{1,0:T(8,128)(2,1)S(1)} %collective-permute-done.4), channel_id=1, source_target_pairs={{0,1},{1,2},{2,3},{3,4},{4,5},{5,6},{6,7},{7,8},{8,9},{9,10},{10,1... | collective-permute-start | bytes 196616 | tf_op jit(solution)/shard_map/ppermute | solution.py:32
  201.7 0.7 copy-start.7
  202.4 6.0 %collective-permute-start.6 = (bf16[512,64]{1,0:T(8,128)(2,1)S(1)}, bf16[512,64]{1,0:T(8,128)(2,1)S(1)}, u32[]{:S(2)}, u32[]{:S(2)}) collective-permute-start(bf16[512,64]{1,0:T(8,128)(2,1)S(1)} %collective-permute-done.5), channel_id=1, source_target_pairs={{0,1},{1,2},{2,3},{3,4},{4,5},{5,6},{6,7},{7,8},{8,9},{9,10},{10,1... | collective-permute-start | bytes 196616 | tf_op jit(solution)/shard_map/ppermute | solution.py:32
  208.4 0.6 copy-start.8
  209.0 5.6 %collective-permute-start.7 = (bf16[512,64]{1,0:T(8,128)(2,1)S(1)}, bf16[512,64]{1,0:T(8,128)(2,1)S(1)}, u32[]{:S(2)}, u32[]{:S(2)}) collective-permute-start(bf16[512,64]{1,0:T(8,128)(2,1)S(1)} %collective-permute-done.6), channel_id=1, source_target_pairs={{0,1},{1,2},{2,3},{3,4},{4,5},{5,6},{6,7},{7,8},{8,9},{9,10},{10,1... | collective-permute-start | bytes 196616 | tf_op jit(solution)/shard_map/ppermute | solution.py:32
  214.6 0.6 copy-start.9
  215.3 5.6 %collective-permute-start.8 = (bf16[512,64]{1,0:T(8,128)(2,1)S(1)}, bf16[512,64]{1,0:T(8,128)(2,1)S(1)}, u32[]{:S(2)}, u32[]{:S(2)}) collective-permute-start(bf16[512,64]{1,0:T(8,128)(2,1)S(1)} %collective-permute-done.7), channel_id=1, source_target_pairs={{0,1},{1,2},{2,3},{3,4},{4,5},{5,6},{6,7},{7,8},{8,9},{9,10},{10,1... | collective-permute-start | bytes 196616 | tf_op jit(solution)/shard_map/ppermute | solution.py:32
  220.9 0.7 copy-start.10
  221.5 5.6 %collective-permute-start.9 = (bf16[512,64]{1,0:T(8,128)(2,1)S(1)}, bf16[512,64]{1,0:T(8,128)(2,1)S(1)}, u32[]{:S(2)}, u32[]{:S(2)}) collective-permute-start(bf16[512,64]{1,0:T(8,128)(2,1)S(1)} %collective-permute-done.8), channel_id=1, source_target_pairs={{0,1},{1,2},{2,3},{3,4},{4,5},{5,6},{6,7},{7,8},{8,9},{9,10},{10,1... | collective-permute-start | bytes 196616 | tf_op jit(solution)/shard_map/ppermute | solution.py:32
  227.1 0.7 copy-start.11
  227.8 5.6 %collective-permute-start.10 = (bf16[512,64]{1,0:T(8,128)(2,1)S(1)}, bf16[512,64]{1,0:T(8,128)(2,1)S(1)}, u32[]{:S(2)}, u32[]{:S(2)}) collective-permute-start(bf16[512,64]{1,0:T(8,128)(2,1)S(1)} %collective-permute-done.9), channel_id=1, source_target_pairs={{0,1},{1,2},{2,3},{3,4},{4,5},{5,6},{6,7},{7,8},{8,9},{9,10},{10,1... | collective-permute-start | bytes 196616 | tf_op jit(solution)/shard_map/ppermute | solution.py:32
  233.4 0.7 copy-start.12
  234.0 5.6 %collective-permute-start.11 = (bf16[512,64]{1,0:T(8,128)(2,1)S(1)}, bf16[512,64]{1,0:T(8,128)(2,1)S(1)}, u32[]{:S(2)}, u32[]{:S(2)}) collective-permute-start(bf16[512,64]{1,0:T(8,128)(2,1)S(1)} %collective-permute-done.10), channel_id=1, source_target_pairs={{0,1},{1,2},{2,3},{3,4},{4,5},{5,6},{6,7},{7,8},{8,9},{9,10},{10,1... | collective-permute-start | bytes 196616 | tf_op jit(solution)/shard_map/ppermute | solution.py:32
  239.6 0.7 copy-start.13
  240.3 5.6 %collective-permute-start.12 = (bf16[512,64]{1,0:T(8,128)(2,1)S(1)}, bf16[512,64]{1,0:T(8,128)(2,1)S(1)}, u32[]{:S(2)}, u32[]{:S(2)}) collective-permute-start(bf16[512,64]{1,0:T(8,128)(2,1)S(1)} %collective-permute-done.11), channel_id=1, source_target_pairs={{0,1},{1,2},{2,3},{3,4},{4,5},{5,6},{6,7},{7,8},{8,9},{9,10},{10,1... | collective-permute-start | bytes 196616 | tf_op jit(solution)/shard_map/ppermute | solution.py:32
  245.9 0.7 copy-start.14
  246.6 5.6 %collective-permute-start.13 = (bf16[512,64]{1,0:T(8,128)(2,1)S(1)}, bf16[512,64]{1,0:T(8,128)(2,1)S(1)}, u32[]{:S(2)}, u32[]{:S(2)}) collective-permute-start(bf16[512,64]{1,0:T(8,128)(2,1)S(1)} %collective-permute-done.12), channel_id=1, source_target_pairs={{0,1},{1,2},{2,3},{3,4},{4,5},{5,6},{6,7},{7,8},{8,9},{9,10},{10,1... | collective-permute-start | bytes 196616 | tf_op jit(solution)/shard_map/ppermute | solution.py:32
  252.2 0.7 copy-start.15
  252.2 5.7 %collective-permute-start.14 = (bf16[512,64]{1,0:T(8,128)(2,1)S(1)}, bf16[512,64]{1,0:T(8,128)(2,1)}, u32[]{:S(2)}, u32[]{:S(2)}) collective-permute-start(bf16[512,64]{1,0:T(8,128)(2,1)S(1)} %collective-permute-done.13), channel_id=1, source_target_pairs={{0,1},{1,2},{2,3},{3,4},{4,5},{5,6},{6,7},{7,8},{8,9},{9,10},{10,1... | collective-permute-start | bytes 196616 | tf_op jit(solution)/shard_map/ppermute | solution.py:32
  279.4 2.4 copy-start.1
  293.7 1.6 copy-start
  296.0 1.0 copy-start.3
Sparse Core Ops, SparseCore 0:
  9.2 46.3 all-gather.2
  61.6 97.4 all-reduce.1
  161.8 45.9 all-gather.4
